TPU v7x, 32 devices: a whole 2x2x4 slice. The times are simulated.
32 devices in a mesh: groups: 2 (over y), ctx: 4 (over z), head: 2 (over x), sub: 2 (over core).
Axes of the slice: x: 2, y: 2, z: 4, core: 2. Of those that a mesh axis runs over, the one named last changes fastest.
Arguments:
- queries: bfloat16 [3072, 8192], P(('groups', 'ctx'), ('head', 'sub')), parts along dimension 0, may hold values from -60 to 60
- key_rows: bfloat16 [3072, 1024], P(('groups', 'ctx'), 'head'), parts along dimension 0, may hold values from -6 to 6
- value_rows: bfloat16 [3072, 1024], P(('groups', 'ctx'), 'head'), parts along dimension 0, may hold values from -6 to 6
- out_weight: bfloat16 [8192, 5120], P(('head', 'sub'), 'ctx'), may hold values from -0.375 to 0.375
Outputs:
- mixed: bfloat16 [3072, 5120], P(('groups', 'ctx'), ('head', 'sub')), parts along dimension 0
There are 2 independent parts, one for each index of `groups`. A program takes and returns all parts, laid end to end along the dimension named above; an argument that names none is the same for every part. Nothing has to cross between parts.
All inputs are finite; a program needn't handle non-finite values.
Results may differ from a plain program's by a relative error of at most 0.02.
Values may be sent and summed in bfloat16 or wider, within the bound.
A program may use at most 128 MiB of HBM per device.

v0:
```python
import functools
import math

import jax
import jax.numpy as jnp
from jax import lax
from jax.experimental import pallas as pl
from jax.experimental.pallas import tpu as pltpu
from jax.sharding import PartitionSpec as P

QH = 64
KVH = 8
HD = 128
CHUNKS = 8
TILE = 256
ROWS = 128
MESH = pl.DeviceIdType.MESH


def kernel(
    n, n_head, per_pair, pairs, chunks, parts, k_hbm, v_hbm, q_hbm, w_hbm, o_ref,
    kv_all, v_ext, q_ref, att, w, own, out, rx1, summed, rx2, final,
    load_sems, kv_send, kv_recv, a_send, a_recv, s1, r1, s2, r2, s3, r3,
):
    me, head, sub = (lax.axis_index(a) for a in ("ctx", "head", "sub"))
    other = 1 - sub
    hs = head * 2 + sub
    tokens, width = q_ref.shape
    heads = width // HD
    columns = w.shape[1]
    piece = width // chunks
    to_right, to_left = me < n - 1, me > 0
    right, left = lax.min(me + 1, n - 1), lax.max(me - 1, 0)
    away = hs != me
    share = tokens // n_head

    def rows_of(b):
        return pl.ds(pl.multiple_of(b * tokens, tokens), tokens)

    first = pl.multiple_of((sub * heads // (QH // KVH)) * HD, HD)
    loads = [
        pltpu.make_async_copy(
            side.at[:, pl.ds(first, pairs * HD)],
            kv_all.at[rows_of(me), pl.ds(i * pairs * HD, pairs * HD)],
            load_sems.at[i],
        )
        for i, side in enumerate((k_hbm, v_hbm))
    ]
    loads.append(pltpu.make_async_copy(q_hbm, q_ref, load_sems.at[2]))
    loads.append(pltpu.make_async_copy(w_hbm, w, load_sems.at[3]))
    for load in loads:
        load.start()

    barrier = pltpu.get_barrier_semaphore()

    def greet(where):
        pl.semaphore_signal(barrier, inc=1, device_id=where, device_id_type=MESH)

    pl.when(to_right)(lambda: greet({"ctx": right}))
    pl.when(to_left)(lambda: greet({"ctx": left}))
    for h in range(n_head):
        source = {"ctx": hs, "head": h, "sub": me % 2}
        pl.when(jnp.logical_or(away, head != h))(functools.partial(greet, source))
    greet({"sub": other})
    for step in range(1, n_head):
        greet({"head": lax.rem(head + step, n_head)})
    count = 2 * n_head - 1 + to_right.astype(jnp.int32) + to_left.astype(jnp.int32)
    pl.semaphore_wait(barrier, count + away.astype(jnp.int32))

    def remote(src, dst, send, recv, where):
        return pltpu.make_async_remote_copy(
            src_ref=src, dst_ref=dst, send_sem=send, recv_sem=recv, device_id=where, device_id_type=MESH
        )

    def kv_copy(b, way, d):
        where = {"ctx": right if way == 0 else left}
        part = kv_all.at[rows_of(b)]
        return remote(part, part, kv_send.at[way, d], kv_recv.at[b], where)

    loads[0].wait()
    loads[1].wait()
    pl.when(to_right)(lambda: kv_copy(me, 0, 0).start())
    pl.when(to_left)(lambda: kv_copy(me, 1, 0).start())

    @pl.loop(1, n)
    def _(d):
        @pl.when(me - d >= 0)
        def _():
            copy = kv_copy(me - d, 0, d)
            copy.wait_recv()
            pl.when(to_right)(lambda: copy.start())

        @pl.when(me + d < n)
        def _():
            copy = kv_copy(me + d, 1, d)
            copy.wait_recv()
            pl.when(to_left)(lambda: copy.start())

    loads[2].wait()

    def a_copy(b, j, way, d):
        where = {"ctx": right if way == 0 else left}
        part = att.at[b, :, pl.ds(j * piece, piece)]
        return remote(part, part, a_send.at[way, d, j], a_recv.at[b, j], where)

    factor = math.log2(math.e) / HD**0.5
    for j in range(chunks):
        if j % (chunks // pairs) == 0:
            p = j // (chunks // pairs)
            v_ext[p, :, :HD] = kv_all[:, (pairs + p) * HD : (pairs + p + 1) * HD]
            v_ext[p, :, HD:] = jnp.ones((v_ext.shape[1], HD), v_ext.dtype)

        @pl.loop(j * heads // chunks, (j + 1) * heads // chunks)
        def _(h):
            pair = h // per_pair
            cols = pl.ds(pl.multiple_of(h * HD, HD), HD)
            keys = kv_all[:, pl.ds(pl.multiple_of(pair * HD, HD), HD)]
            for start in range(0, tokens, ROWS):
                rows = pl.ds(start, ROWS)
                scores = lax.dot_general(
                    q_ref[rows, cols], keys, (((1,), (1,)), ((), ())), preferred_element_type=jnp.float32
                )
                row_max = jnp.max(scores, axis=1, keepdims=True)
                weights = jnp.exp2((scores - row_max) * factor).astype(jnp.bfloat16)
                both = jnp.dot(weights, v_ext[pair], preferred_element_type=jnp.float32)
                att[me, rows, cols] = (both[:, :HD] / both[:, HD:]).astype(att.dtype)

        pl.when(to_right)(lambda: a_copy(me, j, 0, 0).start())
        pl.when(to_left)(lambda: a_copy(me, j, 1, 0).start())

    loads[3].wait()
    tile = columns // parts

    def cols_of(c):
        return pl.ds(0, columns) if parts == 1 else pl.ds(pl.multiple_of(c * tile, tile), tile)

    def core_copy(g, c):
        cols = cols_of(c)
        return remote(out.at[g, :, cols], rx1.at[g, :, cols], s1.at[g, c], r1.at[g, c], {"sub": other})

    def share_of(h):
        return pl.ds(pl.multiple_of(h * share, share), share)

    def head_copy(g, step, c):
        cols, target = cols_of(c), lax.rem(head + step, n_head)
        return remote(
            summed.at[g, share_of(target), cols], rx2.at[g, head, :, cols],
            s2.at[g, step - 1, c], r2.at[g, head, c], {"head": target},
        )

    def head_arrival(g, source, c):
        cols = cols_of(c)
        return remote(
            summed.at[g, share_of(source), cols], rx2.at[g, source, :, cols],
            s2.at[g, 0, c], r2.at[g, source, c], {"head": source},
        )

    def last_copy(g, h, c):
        cols = cols_of(c)
        where = {"ctx": 2 * g + sub, "head": me // 2, "sub": me % 2}
        return remote(final.at[g, :, cols], o_ref.at[share_of(h), cols], s3.at[g, c], r3.at[h, c], where)

    def product(t, c):
        cols = cols_of(c)
        return jnp.dot(att[t], w[:, cols], preferred_element_type=jnp.float32).astype(out.dtype)

    def multiply(t):
        g = t // 2

        @pl.when(t % 2 == sub)
        def _():
            @pl.loop(0, parts)
            def _(c):
                own[g, :, cols_of(c)] = product(t, c)

        @pl.when(t % 2 != sub)
        def _():
            @pl.loop(0, parts)
            def _(c):
                out[g, :, cols_of(c)] = product(t, c)
                core_copy(g, c).start()

    def combine(t):
        g = t // 2

        @pl.when(t % 2 == sub)
        def _():
            @pl.loop(0, parts)
            def _(c):
                cols = cols_of(c)
                core_copy(g, c).wait_recv()
                total = own[g, :, cols].astype(jnp.float32) + rx1[g, :, cols].astype(jnp.float32)
                summed[g, :, cols] = total.astype(summed.dtype)
                for step in range(1, n_head):
                    head_copy(g, step, c).start()

    def finish(t):
        g = t // 2

        @pl.when(t % 2 == sub)
        def _():
            @pl.loop(0, parts)
            def _(c):
                cols = cols_of(c)
                total = summed[g, share_of(head), cols].astype(jnp.float32)
                for step in range(1, n_head):
                    source = lax.rem(head + step, n_head)
                    head_arrival(g, source, c).wait_recv()
                    total += rx2[g, source, :, cols].astype(jnp.float32)
                final[g, :, cols] = total.astype(final.dtype)
                pl.when(jnp.logical_or(away, t != me))(lambda: last_copy(g, head, c).start())

    def finish_at(d):
        pl.when(jnp.logical_and(d >= 0, me - d >= 0))(lambda: finish(me - d))
        pl.when(jnp.logical_and(d > 0, me + d < n))(lambda: finish(me + d))

    def after(d, j, last=False):
        behind, ahead = me - d + 1, me + d - 1
        if j == 0:
            pl.when(behind >= 0)(lambda: multiply(behind))
        if j == chunks // 4:
            pl.when(jnp.logical_and(ahead < n, d > 1))(lambda: multiply(ahead))
        if j == chunks // 2:
            pl.when(behind >= 0)(lambda: combine(behind))
        if j == chunks // 2 + 1:
            pl.when(jnp.logical_and(ahead < n, d > 1))(lambda: combine(ahead))
        if j == chunks - 1 and not last:
            finish_at(d - 2)

    @pl.loop(1, n)
    def _(d):
        for j in range(chunks):

            @pl.when(me - d >= 0)
            def _():
                copy = a_copy(me - d, j, 0, d)
                copy.wait_recv()
                pl.when(to_right)(lambda: copy.start())

            @pl.when(me + d < n)
            def _():
                copy = a_copy(me + d, j, 1, d)
                copy.wait_recv()
                pl.when(to_left)(lambda: copy.start())

            after(d, j)

    finish_at(n - 2)
    for j in range(chunks):
        after(n, j, last=True)
    finish_at(n - 1)

    @pl.when(jnp.logical_not(away))
    def _():
        keep = pltpu.make_async_copy(final.at[me // 2], o_ref.at[share_of(head)], load_sems.at[0])
        keep.start()
        keep.wait()

    for h in range(n_head):

        @pl.when(jnp.logical_or(away, head != h))
        def _():
            @pl.loop(0, parts)
            def _(c):
                last_copy(0, h, c).wait_recv()

    @pl.loop(0, n)
    def _(d):
        for way, fits, go in ((0, me - d >= 0, to_right), (1, me + d < n, to_left)):
            b = me - d if way == 0 else me + d

            @pl.when(jnp.logical_and(fits, go))
            def _():
                kv_copy(b, way, d).wait_send()
                for j in range(chunks):
                    a_copy(b, j, way, d).wait_send()

    @pl.loop(0, n // 2)
    def _(g):
        @pl.loop(0, parts)
        def _(c):
            core_copy(g, c).wait_send()
            for step in range(1, n_head):
                head_copy(g, step, c).wait_send()
            pl.when(jnp.logical_or(away, 2 * g + sub != me))(lambda: last_copy(g, head, c).wait_send())


def on_device(queries, key_rows, value_rows, out_weight):
    tokens, width = queries.shape
    heads_here = width // HD
    group_ratio = QH // KVH
    pairs = max(heads_here // group_ratio, 1)
    per_pair = heads_here // pairs
    n = lax.axis_size("ctx")
    n_head = lax.axis_size("head")
    columns = out_weight.shape[1]
    block = (tokens, columns)
    groups = (n // 2,) + block
    chunks = min(CHUNKS, heads_here)
    parts = columns // TILE if columns % TILE == 0 else 1
    anywhere = pl.BlockSpec(memory_space=pl.ANY)
    dma = pltpu.SemaphoreType.DMA
    bf16 = jnp.bfloat16
    return pl.pallas_call(
        functools.partial(kernel, n, n_head, per_pair, pairs, chunks, parts),
        out_shape=jax.ShapeDtypeStruct(block, bf16),
        in_specs=[anywhere] * 4,
        out_specs=anywhere,
        scratch_shapes=[
            pltpu.VMEM((n * tokens, 2 * pairs * HD), bf16),
            pltpu.VMEM((pairs, n * tokens, 2 * HD), bf16),
            pltpu.VMEM((tokens, width), bf16),
            pltpu.VMEM((n, tokens, width), bf16),
            pltpu.VMEM(out_weight.shape, bf16),
            pltpu.VMEM(groups, bf16),
            pltpu.VMEM(groups, bf16),
            pltpu.VMEM(groups, bf16),
            pltpu.VMEM(groups, bf16),
            pltpu.VMEM((n // 2, n_head, tokens // n_head, columns), bf16),
            pltpu.VMEM((n // 2, tokens // n_head, columns), bf16),
            dma((4,)),
            dma((2, n)),
            dma((n,)),
            dma((2, n, chunks)),
            dma((n, chunks)),
            dma((n // 2, parts)),
            dma((n // 2, parts)),
            dma((n // 2, n_head - 1, parts)),
            dma((n // 2, n_head, parts)),
            dma((n // 2, parts)),
            dma((n_head, parts)),
        ],
        compiler_params=pltpu.CompilerParams(
            collective_id=0, has_side_effects=True, vmem_limit_bytes=60 * 2**20
        ),
    )(key_rows, value_rows, queries, out_weight)


def solution(mesh):
    assert mesh.shape["sub"] == 2
    assert mesh.shape["ctx"] == mesh.shape["head"] * mesh.shape["sub"]
    return jax.shard_map(
        on_device,
        mesh=mesh,
        in_specs=(
            P(("groups", "ctx"), ("head", "sub")),
            P(("groups", "ctx"), "head"),
            P(("groups", "ctx"), "head"),
            P(("head", "sub"), "ctx"),
        ),
        out_specs=P(("groups", "ctx"), ("head", "sub")),
        check_vma=False,
    )
```

profile of v0, /device:TPU:24, one launch (start us, length us, event | category | flops | bytes accessed | tf_op | source)
XLA Modules:
  0.0 167.0 jit_solution(10364317827790260050)
XLA Ops:
  0.0 164.8 %shard_map.46 = bf16[384,1280]{1,0:T(8,128)(2,1)} custom-call(bf16[384,512]{1,0:T(8,128)(2,1)} %k_hbm.1, bf16[384,512]{1,0:T(8,128)(2,1)} %v_hbm.1, bf16[384,2048]{1,0:T(8,128)(2,1)} %q_hbm.1, bf16[2048,1280]{1,0:T(8,128)(2,1)} %w_hbm.1), custom_call_target="tpu_custom_call" | custom-call | tf_op jit(solution)/shard_map/pallas_call | solution.py:304
  164.8 2.2 %copy.6 = bf16[384,1280]{1,0:T(8,128)(2,1)} copy(bf16[384,1280]{1,0:T(8,128)(2,1)} %shard_map.46) | data formatting | bytes 1966080
where the time goes:
time: 167 us
  Pallas kernels  165 us (99%)
  local copies, waits for them, and re-layouts  2.21 us (1%)
    pallas_call x1, Pallas kernels, on_device(): pl.pallas_call(functools.partial(kernel, n, n_head, per_pair, pairs, chun...  165 us

commit v1 on v0

--- a/solution.py
+++ b/solution.py
@@ -15,6 +15,9 @@
 TILE = 256
 ROWS = 128
 MESH = pl.DeviceIdType.MESH
+BLOCK = 128
+EARLY = 2
+ORDER = ("w", "w", "w", "w", "w", 0, 1, "w", "w", 2, "w", "w", "w")
 
 
 def kernel(
@@ -336,18 +339,526 @@
     )(key_rows, value_rows, queries, out_weight)
 
 
+def hub_kernel(
+    n, n_head, per_pair, pairs, chunks, tile, k_hbm, v_hbm, q_hbm, w_hbm, o_ref,
+    kv_all, v_ext, q_ref, att, w, w_far, part, rx1, rx2,
+    load_sems, kv_send, kv_recv, a_send, a_recv, e_send, e_recv, f_send, f_recv,
+    w_send, w_recv, y_send, y_recv, s1, r1, s2, r2, s3, r3,
+):
+    me, head, sub, group = (lax.axis_index(a) for a in ("ctx", "head", "sub", "groups"))
+    tokens, width = q_ref.shape
+    heads = width // HD
+    columns = w.shape[1]
+    blocks = tokens // BLOCK
+    tiles = columns // tile
+    pieces = 2 * tiles
+    per_piece = width // 4
+    low = n // 2 - 1
+    is_hub = jnp.logical_and(me >= low, me <= low + 1)
+    is_end = jnp.logical_not(is_hub)
+    to_right, to_left = me < n - 1, me > 0
+    right, left = lax.min(me + 1, n - 1), lax.max(me - 1, 0)
+    other = n - 1 - me
+    end = jnp.where(me <= low, 0, n - 1)
+    far_end = n - 1 - end
+    my_hub = jnp.where(me <= low, low, low + 1)
+    side = me - low
+    away_head, away_sub, away_group = 1 - head, 1 - sub, 1 - group
+
+    def rows_of(b):
+        return pl.ds(pl.multiple_of(b * tokens, tokens), tokens)
+
+    first = pl.multiple_of((sub * heads // (QH // KVH)) * HD, HD)
+    loads = []
+    for p in range(pairs):
+        for i, ref in enumerate((k_hbm, v_hbm)):
+            loads.append(pltpu.make_async_copy(
+                ref.at[:, pl.ds(pl.multiple_of(first + p * HD, HD), HD)],
+                kv_all.at[rows_of(me), pl.ds((2 * p + i) * HD, HD)],
+                load_sems.at[2 * p + i],
+            ))
+    load_w = pltpu.make_async_copy(w_hbm, w, load_sems.at[2 * pairs])
+    load_q = pltpu.make_async_copy(q_hbm, q_ref, load_sems.at[2 * pairs + 1])
+    for load in loads + [load_w, load_q]:
+        load.start()
+
+    barrier = pltpu.get_barrier_semaphore()
+
+    def greet(where):
+        pl.semaphore_signal(barrier, inc=1, device_id=where, device_id_type=MESH)
+
+    pl.when(to_right)(lambda: greet({"ctx": right}))
+    pl.when(to_left)(lambda: greet({"ctx": left}))
+    greet({"sub": away_sub})
+    greet({"head": away_head})
+    greet({"groups": away_group})
+    origin = low + head
+    mine = jnp.logical_and(me == origin, sub == me % 2)
+    for h in range(n_head):
+        source = {"ctx": origin, "head": h, "sub": me % 2}
+        pl.when(jnp.logical_not(jnp.logical_and(mine, head == h)))(functools.partial(greet, source))
+    keeps = jnp.logical_and(is_hub, jnp.logical_and(head == side, sub == me % 2))
+    count = 3 + to_right.astype(jnp.int32) + to_left.astype(jnp.int32)
+    count += jnp.where(is_hub, 4, 0) - keeps.astype(jnp.int32)
+    pl.semaphore_wait(barrier, count)
+
+    def remote(src, dst, send, recv, where):
+        return pltpu.make_async_remote_copy(
+            src_ref=src, dst_ref=dst, send_sem=send, recv_sem=recv, device_id=where, device_id_type=MESH
+        )
+
+    def kv_copy(b, way, d, p):
+        where = {"ctx": right if way == 0 else left}
+        block = kv_all.at[rows_of(b), pl.ds(2 * p * HD, 2 * HD)]
+        return remote(block, block, kv_send.at[way, d, p], kv_recv.at[b, p], where)
+
+    for p in range(pairs):
+        loads[2 * p].wait()
+        loads[2 * p + 1].wait()
+        pl.when(to_right)(lambda: kv_copy(me, 0, 0, p).start())
+        pl.when(to_left)(lambda: kv_copy(me, 1, 0, p).start())
+
+    def pass_on(d, p):
+        @pl.when(me - d >= 0)
+        def _():
+            copy = kv_copy(me - d, 0, d, p)
+            copy.wait_recv()
+            pl.when(to_right)(lambda: copy.start())
+
+        @pl.when(me + d < n)
+        def _():
+            copy = kv_copy(me + d, 1, d, p)
+            copy.wait_recv()
+            pl.when(to_left)(lambda: copy.start())
+
+    def w_piece(g, i):
+        rows = pl.ds(pl.multiple_of(g * (width // 2) + (i % 2) * per_piece, per_piece), per_piece)
+        return rows, pl.ds((i // 2) * tile, tile)
+
+    def w_copy(i):
+        at = w_piece(group, i)
+        return remote(w.at[at], w_far.at[at], w_send.at[i], w_recv.at[i], {"ctx": my_hub})
+
+    def y_copy(g, i):
+        at = w_piece(g, i)
+        return remote(w_far.at[at], w_far.at[at], y_send.at[i], y_recv.at[i], {"groups": away_group})
+
+    def relay_w(*which):
+        for i in which:
+            w_copy(i).wait_recv()
+            y_copy(group, i).start()
+
+    def await_w(*which):
+        for i in which:
+            y_copy(away_group, i).wait_recv()
+
+    load_w.wait()
+    ahead = ORDER.index(0)
+
+    @pl.when(is_end)
+    def _():
+        for i in range(ahead):
+            w_copy(i).start()
+
+    chunk = width // chunks
+
+    def chunk_copy(b, j):
+        at = att.at[b, :, pl.ds(j * chunk, chunk)]
+        return remote(at, at, a_send.at[j], a_recv.at[j], {"ctx": other})
+
+    def end_copy(r):
+        at = att.at[end, pl.ds(r * BLOCK, BLOCK)]
+        return remote(at, at, e_send.at[r], e_recv.at[r], {"ctx": my_hub})
+
+    def far_copy(b, r):
+        at = att.at[b, pl.ds(r * BLOCK, BLOCK)]
+        return remote(at, at, f_send.at[r], f_recv.at[r], {"ctx": other})
+
+    for d in range(1, n):
+        pass_on(d, 0)
+        if d == 1:
+            for p in range(1, pairs):
+                pass_on(d, p)
+    load_q.wait()
+
+    factor = math.log2(math.e) / HD**0.5
+    per_chunk = heads // chunks
+    for j in range(chunks):
+        if (j * per_chunk) % per_pair == 0:
+            p = j * per_chunk // per_pair
+            v_ext[:, :HD] = kv_all[:, (2 * p + 1) * HD : (2 * p + 2) * HD]
+            if p == 0:
+                v_ext[:, HD:] = jnp.ones((v_ext.shape[0], HD), v_ext.dtype)
+        p = j * per_chunk // per_pair
+        keys_at = pl.ds(2 * p * HD, HD)
+
+        @pl.loop(j * per_chunk, (j + 1) * per_chunk)
+        def _(h):
+            cols = pl.ds(pl.multiple_of(h * HD, HD), HD)
+            keys = kv_all[:, keys_at]
+            for start in range(0, tokens, ROWS):
+                rows = pl.ds(start, ROWS)
+                scores = lax.dot_general(
+                    q_ref[rows, cols], keys, (((1,), (1,)), ((), ())), preferred_element_type=jnp.float32
+                )
+                row_max = jnp.max(scores, axis=1, keepdims=True)
+                weights = jnp.exp2((scores - row_max) * factor).astype(jnp.bfloat16)
+                both = jnp.dot(weights, v_ext[...], preferred_element_type=jnp.float32)
+                att[me, rows, cols] = (both[:, :HD] / both[:, HD:]).astype(att.dtype)
+
+        pl.when(is_hub)(functools.partial(lambda j: chunk_copy(me, j).start(), j))
+        if j == 1:
+            for d in range(2, n):
+                for p in range(1, pairs):
+                    pass_on(d, p)
+        if j % 2 == 1:
+            pl.when(is_hub)(functools.partial(relay_w, j // 2))
+
+    @pl.when(is_end)
+    def _():
+        i = ahead
+        for what in ORDER[ahead:]:
+            if what == "w":
+                w_copy(i).start()
+                i += 1
+            else:
+                end_copy(what).start()
+
+    late = tiles - EARLY
+
+    def geometry(kind, r):
+        if kind == "near":
+            return 0, r * BLOCK, BLOCK, 0, tiles, r
+        if kind == "early":
+            return 1, r * BLOCK, BLOCK, 0, EARLY, blocks + r
+        return 1, 0, tokens, r, 1, 2 * blocks + r - EARLY
+
+    def region(kind, r, half=None):
+        cb, row, m, c, k, index = geometry(kind, r)
+        if half is not None:
+            row, m = row + half * (m // 2), m // 2
+            row = row if isinstance(row, int) else pl.multiple_of(row, m)
+        return cb, pl.ds(row, m), pl.ds(c * tile, k * tile), index
+
+    def product(t, row, m, cb, c, k):
+        source = w_far if cb else w
+
+        @pl.loop(c, c + k)
+        def _(i):
+            cols = pl.ds(pl.multiple_of(i * tile, tile), tile)
+            part[t, cb, pl.ds(row, m), cols] = jnp.dot(
+                att[t, pl.ds(row, m)], source[:, cols], preferred_element_type=jnp.float32
+            ).astype(part.dtype)
+
+    def core_copy(t, kind, r):
+        cb, rows, cols, index = region(kind, r)
+        return remote(
+            part.at[t, cb, rows, cols], rx1.at[t // 2, cb, rows, cols],
+            s1.at[t // 2, index], r1.at[t // 2, index], {"sub": away_sub},
+        )
+
+    def head_copy(t, kind, r):
+        cb, rows, cols, index = region(kind, r, away_head)
+        half, short = geometry(kind, r)[1] // 2, geometry(kind, r)[2] // 2
+        return remote(
+            part.at[t, cb, rows, cols], rx2.at[t // 2, cb, pl.ds(half, short), cols],
+            s2.at[t // 2, index], r2.at[t // 2, index], {"head": away_head},
+        )
+
+    def is_kept(t, cb):
+        if cb:
+            return jnp.bool_(False)
+        return jnp.logical_and(t == me, keeps)
+
+    def last_copy(t, kind, r):
+        cb, rows, cols, index = region(kind, r, head)
+        where = {"ctx": t, "head": side, "sub": (me + cb) % 2}
+        return remote(
+            part.at[t, cb, rows, cols], o_ref.at[rows, cols], s3.at[t // 2, index], r3.at[head, index], where
+        )
+
+    def keep_copy(t, kind, r):
+        cb, rows, cols, index = region(kind, r, head)
+        return pltpu.make_async_copy(part.at[t, cb, rows, cols], o_ref.at[rows, cols], s3.at[t // 2, index])
+
+    def owns(t):
+        return t % 2 == sub
+
+    def send(jobs):
+        for t, kind, r in jobs:
+            pl.when(jnp.logical_not(owns(t)))(functools.partial(lambda *a: core_copy(*a).start(), t, kind, r))
+
+    def multiply(*jobs):
+        for t, kind, r in jobs:
+            cb, row, m, c, k, _ = geometry(kind, r)
+            product(t, row, m, cb, c, k)
+            send([(t, kind, r)])
+
+    def multiply_all(t, kind):
+        cb, _, _, c, k, _ = geometry(kind, 0)
+        product(t, 0, tokens, cb, c, k)
+        send([(t, kind, r) for r in range(blocks)])
+
+    def combine(*jobs):
+        for t, kind, r in jobs:
+
+            @pl.when(owns(t))
+            def _():
+                cb, rows, cols, _ = region(kind, r)
+                core_copy(t, kind, r).wait_recv()
+                total = part[t, cb, rows, cols].astype(jnp.float32)
+                total += rx1[t // 2, cb, rows, cols].astype(jnp.float32)
+                part[t, cb, rows, cols] = total.astype(part.dtype)
+                head_copy(t, kind, r).start()
+
+    def finish(*jobs):
+        for t, kind, r in jobs:
+
+            @pl.when(owns(t))
+            def _():
+                cb, rows, cols, _ = region(kind, r, head)
+                half, short = geometry(kind, r)[1] // 2, geometry(kind, r)[2] // 2
+                head_copy(t, kind, r).wait_recv()
+                total = part[t, cb, rows, cols].astype(jnp.float32)
+                total += rx2[t // 2, cb, pl.ds(half, short), cols].astype(jnp.float32)
+                part[t, cb, rows, cols] = total.astype(part.dtype)
+                if cb:
+                    last_copy(t, kind, r).start()
+                else:
+                    pl.when(is_kept(t, cb))(lambda: keep_copy(t, kind, r).start())
+                    pl.when(jnp.logical_not(is_kept(t, cb)))(lambda: last_copy(t, kind, r).start())
+
+    def relay_end(r):
+        end_copy(r).wait_recv()
+        far_copy(end, r).start()
+
+    def await_far(r):
+        far_copy(far_end, r).wait_recv()
+
+    def all_rows(t, kind):
+        return [(t, kind, r) for r in range(blocks)]
+
+    def both(t, r):
+        return [(t, "near", r), (t, "early", r)]
+
+    @pl.when(is_hub)
+    def _():
+        g0, g1 = all_rows(me, "near"), all_rows(me, "early")
+        g2, g5, g9 = both(end, 0), both(end, 1), both(end, 2)
+        g3, g4 = all_rows(other, "near"), all_rows(other, "early")
+        g6, g7, g11 = both(far_end, 0), both(far_end, 1), both(far_end, 2)
+
+        def late_of(i, *toks):
+            return [(t, "late", i) for t in toks]
+
+        multiply_all(me, "near")
+        relay_w(4)
+        await_w(0, 1, 2, 3)
+        multiply_all(me, "early")
+        combine(*g0)
+        combine(*g1)
+        relay_end(0)
+        multiply(*g2)
+        finish(*g0)
+        finish(*g1)
+        combine(*g2)
+        for j in range(chunks):
+            chunk_copy(other, j).wait_recv()
+        multiply_all(other, "near")
+        multiply_all(other, "early")
+        combine(*g3)
+        combine(*g4)
+        finish(*g2)
+        relay_end(1)
+        multiply(*g5)
+        await_far(0)
+        multiply(*g6)
+        combine(*g5)
+        finish(*g3)
+        finish(*g4)
+        combine(*g6)
+        relay_w(5)
+        finish(*g5)
+        relay_w(6)
+        finish(*g6)
+        await_far(1)
+        multiply(*g7)
+        await_w(4, 5)
+        g8 = late_of(2, me, other)
+        multiply(*g8)
+        combine(*g7)
+        combine(*g8)
+        finish(*g7)
+        relay_end(2)
+        multiply(*g9)
+        g9 = g9 + late_of(2, end)
+        multiply(*g9[2:])
+        finish(*g8)
+        combine(*g9)
+        relay_w(7)
+        finish(*g9)
+        relay_w(8)
+        await_w(6, 7)
+        g10 = late_of(3, me, other, end)
+        multiply(*g10)
+        await_far(2)
+        g11 = g11 + late_of(2, far_end) + late_of(3, far_end)
+        multiply(*g11)
+        combine(*g10)
+        combine(*g11)
+        relay_w(9)
+        finish(*g10)
+        finish(*g11)
+        await_w(8, 9)
+        g13 = late_of(4, far_end, other, end, me)
+        multiply(*g13)
+        combine(*g13)
+        finish(*g13)
+
+    my_cb = (sub + 1 + head) % 2
+
+    def arrivals(cb):
+        kinds = [("near", r) for r in range(blocks)]
+        if cb:
+            kinds = [("early", r) for r in range(blocks)] + [("late", r) for r in range(EARLY, tiles)]
+        for kind, r in kinds:
+            for h in range(n_head):
+                cb_, rows, cols, index = region(kind, r, h)
+                got = remote(
+                    part.at[0, cb_, rows, cols], o_ref.at[rows, cols], s3.at[0, index], r3.at[h, index],
+                    {"ctx": origin, "head": h, "sub": me % 2},
+                )
+                if cb:
+                    got.wait_recv()
+                else:
+                    pl.when(jnp.logical_not(jnp.logical_and(mine, head == h)))(lambda: got.wait_recv())
+
+    pl.when(my_cb == 0)(lambda: arrivals(0))
+    pl.when(my_cb == 1)(lambda: arrivals(1))
+
+    for way, go in ((0, to_right), (1, to_left)):
+        for d in range(n):
+            b = me - d if way == 0 else me + d
+            fits = b >= 0 if way == 0 else b < n
+
+            @pl.when(jnp.logical_and(fits, go))
+            def _():
+                for p in range(pairs):
+                    kv_copy(b, way, d, p).wait_send()
+
+    @pl.when(is_end)
+    def _():
+        for i in range(pieces):
+            w_copy(i).wait_send()
+        for r in range(blocks):
+            end_copy(r).wait_send()
+
+    @pl.when(is_hub)
+    def _():
+        for i in range(pieces):
+            y_copy(group, i).wait_send()
+        for j in range(chunks):
+            chunk_copy(me, j).wait_send()
+        for r in range(blocks):
+            far_copy(end, r).wait_send()
+        names = [("near", r) for r in range(blocks)] + [("early", r) for r in range(blocks)]
+        names += [("late", r) for r in range(EARLY, tiles)]
+        for t in (me, other, end, far_end):
+            for kind, r in names:
+
+                @pl.when(owns(t))
+                def _():
+                    head_copy(t, kind, r).wait_send()
+                    if kind == "near":
+                        kept = is_kept(t, 0)
+                        pl.when(kept)(lambda: keep_copy(t, kind, r).wait())
+                        pl.when(jnp.logical_not(kept))(lambda: last_copy(t, kind, r).wait_send())
+                    else:
+                        last_copy(t, kind, r).wait_send()
+
+                @pl.when(jnp.logical_not(owns(t)))
+                def _():
+                    core_copy(t, kind, r).wait_send()
+
+
+def with_hubs(queries, key_rows, value_rows, out_weight):
+    tokens, width = queries.shape
+    heads_here = width // HD
+    pairs = heads_here // (QH // KVH)
+    per_pair = heads_here // pairs
+    n = lax.axis_size("ctx")
+    n_head = lax.axis_size("head")
+    columns = out_weight.shape[1]
+    block = (tokens, columns)
+    tiles = columns // TILE
+    pieces = 2 * tiles
+    blocks = tokens // BLOCK
+    kinds = 2 * blocks + tiles - EARLY
+    anywhere = pl.BlockSpec(memory_space=pl.ANY)
+    dma = pltpu.SemaphoreType.DMA
+    bf16 = jnp.bfloat16
+    sums = [dma((n // 2, kinds))] * 5 + [dma((n_head, kinds))]
+    return pl.pallas_call(
+        functools.partial(hub_kernel, n, n_head, per_pair, pairs, CHUNKS, TILE),
+        out_shape=jax.ShapeDtypeStruct(block, bf16),
+        in_specs=[anywhere] * 4,
+        out_specs=anywhere,
+        scratch_shapes=[
+            pltpu.VMEM((n * tokens, 2 * pairs * HD), bf16),
+            pltpu.VMEM((n * tokens, 2 * HD), bf16),
+            pltpu.VMEM((tokens, width), bf16),
+            pltpu.VMEM((n, tokens, width), bf16),
+            pltpu.VMEM(out_weight.shape, bf16),
+            pltpu.VMEM(out_weight.shape, bf16),
+            pltpu.VMEM((n, 2) + block, bf16),
+            pltpu.VMEM((n // 2, 2) + block, bf16),
+            pltpu.VMEM((n // 2, 2, tokens // 2, columns), bf16),
+            dma((2 * pairs + 2,)),
+            dma((2, n, pairs)),
+            dma((n, pairs)),
+            dma((CHUNKS,)),
+            dma((CHUNKS,)),
+            dma((blocks,)),
+            dma((blocks,)),
+            dma((blocks,)),
+            dma((blocks,)),
+            dma((pieces,)),
+            dma((pieces,)),
+            dma((pieces,)),
+            dma((pieces,)),
+        ] + sums,
+        compiler_params=pltpu.CompilerParams(
+            collective_id=0, has_side_effects=True, vmem_limit_bytes=60 * 2**20
+        ),
+    )(key_rows, value_rows, queries, out_weight)
+
+
+def hubs_fit(mesh, queries, out_weight):
+    shape = mesh.shape
+    tokens, width = queries[0] // (shape["groups"] * shape["ctx"]), queries[1] // (shape["head"] * shape["sub"])
+    columns = out_weight[1] // shape["ctx"]
+    sizes = (shape["groups"], shape["ctx"], shape["head"], shape["sub"]) == (2, 4, 2, 2)
+    heads = width // HD
+    return sizes and tokens == 3 * BLOCK and columns == 5 * TILE and heads == 2 * CHUNKS and heads * KVH == 2 * QH
+
+
 def solution(mesh):
     assert mesh.shape["sub"] == 2
     assert mesh.shape["ctx"] == mesh.shape["head"] * mesh.shape["sub"]
-    return jax.shard_map(
-        on_device,
-        mesh=mesh,
-        in_specs=(
-            P(("groups", "ctx"), ("head", "sub")),
-            P(("groups", "ctx"), "head"),
-            P(("groups", "ctx"), "head"),
-            P(("head", "sub"), "ctx"),
-        ),
-        out_specs=P(("groups", "ctx"), ("head", "sub")),
-        check_vma=False,
-    )
+
+    def run(queries, key_rows, value_rows, out_weight):
+        fits = hubs_fit(mesh, queries.shape, out_weight.shape)
+        return jax.shard_map(
+            with_hubs if fits else on_device,
+            mesh=mesh,
+            in_specs=(
+                P(("groups", "ctx"), ("head", "sub")),
+                P(("groups", "ctx"), "head"),
+                P(("groups", "ctx"), "head"),
+                P(("head", "sub"), "ctx"),
+            ),
+            out_specs=P(("groups", "ctx"), ("head", "sub")),
+            check_vma=False,
+        )(queries, key_rows, value_rows, out_weight)
+
+    return run

time: 167 us -> 146 us (0.87)
  the two profiles are of different devices: /device:TPU:24 before, /device:TPU:0 now
where the time goes in v1:
time: 146 us
  Pallas kernels  144 us (99%)
  local copies, waits for them, and re-layouts  2.21 us (2%)
    pallas_call x1, Pallas kernels, with_hubs(): pl.pallas_call(functools.partial(hub_kernel, n, n_head, per_pair, pairs,...  144 us

profile of v1, /device:TPU:0, one launch (start us, length us, event | category | flops | bytes accessed | tf_op | source)
XLA Modules:
  0.0 145.8 jit_solution(11112911030388017562)
XLA Ops:
  0.0 143.6 %shard_map.46 = bf16[384,1280]{1,0:T(8,128)(2,1)} custom-call(bf16[384,512]{1,0:T(8,128)(2,1)} %k_hbm.1, bf16[384,512]{1,0:T(8,128)(2,1)} %v_hbm.1, bf16[384,2048]{1,0:T(8,128)(2,1)} %q_hbm.1, bf16[2048,1280]{1,0:T(8,128)(2,1)} %w_hbm.1), custom_call_target="tpu_custom_call" | custom-call | tf_op jit(solution)/shard_map/pallas_call | solution.py:801
  143.6 2.2 %copy.6 = bf16[384,1280]{1,0:T(8,128)(2,1)} copy(bf16[384,1280]{1,0:T(8,128)(2,1)} %shard_map.46) | data formatting | bytes 1966080

commit v2 on v1

--- a/solution.py
+++ b/solution.py
@@ -17,7 +17,9 @@
 MESH = pl.DeviceIdType.MESH
 BLOCK = 128
 EARLY = 2
-ORDER = ("w", "w", "w", "w", "w", 0, 1, "w", "w", 2, "w", "w", "w")
+SPLIT = 4
+TOGETHER = 4
+ORDER = ("w",) * 8 + (0, 1, 2) + ("w",) * 12
 
 
 def kernel(
@@ -351,8 +353,8 @@
     columns = w.shape[1]
     blocks = tokens // BLOCK
     tiles = columns // tile
-    pieces = 2 * tiles
-    per_piece = width // 4
+    pieces = SPLIT * tiles
+    per_piece = width // (2 * SPLIT)
     low = n // 2 - 1
     is_hub = jnp.logical_and(me >= low, me <= low + 1)
     is_end = jnp.logical_not(is_hub)
@@ -432,8 +434,8 @@
             pl.when(to_left)(lambda: copy.start())
 
     def w_piece(g, i):
-        rows = pl.ds(pl.multiple_of(g * (width // 2) + (i % 2) * per_piece, per_piece), per_piece)
-        return rows, pl.ds((i // 2) * tile, tile)
+        rows = pl.ds(pl.multiple_of(g * (width // 2) + (i % SPLIT) * per_piece, per_piece), per_piece)
+        return rows, pl.ds((i // SPLIT) * tile, tile)
 
     def w_copy(i):
         at = w_piece(group, i)
@@ -483,46 +485,68 @@
 
     factor = math.log2(math.e) / HD**0.5
     per_chunk = heads // chunks
-    for j in range(chunks):
-        if (j * per_chunk) % per_pair == 0:
+
+    def prepare(p):
+        v_ext[p, :, :HD] = kv_all[:, (2 * p + 1) * HD : (2 * p + 2) * HD]
+        v_ext[p, :, HD:] = jnp.ones((v_ext.shape[1], HD), v_ext.dtype)
+
+    def attend(h, p, start):
+        rows, cols = pl.ds(start, ROWS), pl.ds(pl.multiple_of(h * HD, HD), HD)
+        keys = kv_all[:, 2 * p * HD : (2 * p + 1) * HD]
+        scores = lax.dot_general(
+            q_ref[rows, cols], keys, (((1,), (1,)), ((), ())), preferred_element_type=jnp.float32
+        )
+        row_max = jnp.max(scores, axis=1, keepdims=True)
+        weights = jnp.exp2((scores - row_max) * factor).astype(jnp.bfloat16)
+        both = jnp.dot(weights, v_ext[p], preferred_element_type=jnp.float32)
+        att[me, rows, cols] = (both[:, :HD] / both[:, HD:]).astype(att.dtype)
+
+    def rest_of_pairs():
+        for d in range(2, n):
+            for p in range(1, pairs):
+                pass_on(d, p)
+
+    @pl.when(is_hub)
+    def _():
+        relay_w(0)
+        for j in range(chunks):
             p = j * per_chunk // per_pair
-            v_ext[:, :HD] = kv_all[:, (2 * p + 1) * HD : (2 * p + 2) * HD]
-            if p == 0:
-                v_ext[:, HD:] = jnp.ones((v_ext.shape[0], HD), v_ext.dtype)
-        p = j * per_chunk // per_pair
-        keys_at = pl.ds(2 * p * HD, HD)
-
-        @pl.loop(j * per_chunk, (j + 1) * per_chunk)
-        def _(h):
-            cols = pl.ds(pl.multiple_of(h * HD, HD), HD)
-            keys = kv_all[:, keys_at]
-            for start in range(0, tokens, ROWS):
-                rows = pl.ds(start, ROWS)
-                scores = lax.dot_general(
-                    q_ref[rows, cols], keys, (((1,), (1,)), ((), ())), preferred_element_type=jnp.float32
-                )
-                row_max = jnp.max(scores, axis=1, keepdims=True)
-                weights = jnp.exp2((scores - row_max) * factor).astype(jnp.bfloat16)
-                both = jnp.dot(weights, v_ext[...], preferred_element_type=jnp.float32)
-                att[me, rows, cols] = (both[:, :HD] / both[:, HD:]).astype(att.dtype)
-
-        pl.when(is_hub)(functools.partial(lambda j: chunk_copy(me, j).start(), j))
-        if j == 1:
-            for d in range(2, n):
-                for p in range(1, pairs):
-                    pass_on(d, p)
-        if j % 2 == 1:
-            pl.when(is_hub)(functools.partial(relay_w, j // 2))
+            if (j * per_chunk) % per_pair == 0:
+                prepare(p)
+
+            @pl.loop(j * per_chunk, (j + 1) * per_chunk)
+            def _(h):
+                for start in range(0, tokens, ROWS):
+                    attend(h, p, start)
+
+            chunk_copy(me, j).start()
+            if j == 1:
+                rest_of_pairs()
+            if j + 1 < chunks:
+                relay_w(j + 1)
 
     @pl.when(is_end)
     def _():
         i = ahead
-        for what in ORDER[ahead:]:
-            if what == "w":
+        prepare(0)
+        for r in range(blocks):
+            for p in range(pairs):
+                if r == 0 and p == 1:
+                    rest_of_pairs()
+                    for q in range(1, pairs):
+                        prepare(q)
+
+                @pl.loop(p * per_pair, (p + 1) * per_pair, step=TOGETHER)
+                def _(h):
+                    for k in range(TOGETHER):
+                        for start in range(r * BLOCK, (r + 1) * BLOCK, ROWS):
+                            attend(h + k, p, start)
+
+            end_copy(r).start()
+            after = ORDER.index(r) + 1
+            while after < len(ORDER) and ORDER[after] == "w":
                 w_copy(i).start()
-                i += 1
-            else:
-                end_copy(what).start()
+                i, after = i + 1, after + 1
 
     late = tiles - EARLY
 
@@ -651,68 +675,76 @@
         def late_of(i, *toks):
             return [(t, "late", i) for t in toks]
 
+        g8, g10 = late_of(2, me, other, end), late_of(3, far_end, other, end, me)
+        g11 = g11 + late_of(2, far_end)
+        g12, g13 = late_of(4, far_end, other), late_of(4, end, me)
+
         multiply_all(me, "near")
-        relay_w(4)
-        await_w(0, 1, 2, 3)
+        await_w(*range(8))
         multiply_all(me, "early")
         combine(*g0)
         combine(*g1)
         relay_end(0)
         multiply(*g2)
+        combine(*g2)
         finish(*g0)
         finish(*g1)
-        combine(*g2)
         for j in range(chunks):
             chunk_copy(other, j).wait_recv()
         multiply_all(other, "near")
+        relay_end(1)
         multiply_all(other, "early")
         combine(*g3)
         combine(*g4)
+        multiply(*g5)
         finish(*g2)
-        relay_end(1)
-        multiply(*g5)
+        combine(*g5)
         await_far(0)
         multiply(*g6)
-        combine(*g5)
+        relay_end(2)
+        combine(*g6)
+        multiply(*g9)
+        relay_w(8)
+        combine(*g9)
         finish(*g3)
+        relay_w(9)
         finish(*g4)
-        combine(*g6)
-        relay_w(5)
+        relay_w(10)
         finish(*g5)
-        relay_w(6)
-        finish(*g6)
         await_far(1)
         multiply(*g7)
-        await_w(4, 5)
-        g8 = late_of(2, me, other)
+        relay_w(11)
+        combine(*g7)
+        finish(*g6)
+        relay_w(12)
+        await_w(8, 9, 10, 11)
         multiply(*g8)
-        combine(*g7)
+        relay_w(13)
         combine(*g8)
+        finish(*g9)
+        await_far(2)
+        relay_w(14)
+        multiply(*g11)
+        relay_w(15)
+        combine(*g11)
         finish(*g7)
-        relay_end(2)
-        multiply(*g9)
-        g9 = g9 + late_of(2, end)
-        multiply(*g9[2:])
+        relay_w(16)
+        await_w(12, 13, 14, 15)
+        multiply(*g10[:2])
+        relay_w(17)
+        multiply(*g10[2:])
+        relay_w(18)
+        combine(*g10)
         finish(*g8)
-        combine(*g9)
-        relay_w(7)
-        finish(*g9)
-        relay_w(8)
-        await_w(6, 7)
-        g10 = late_of(3, me, other, end)
-        multiply(*g10)
-        await_far(2)
-        g11 = g11 + late_of(2, far_end) + late_of(3, far_end)
-        multiply(*g11)
-        combine(*g10)
-        combine(*g11)
-        relay_w(9)
+        finish(*g11)
+        relay_w(19)
         finish(*g10)
-        finish(*g11)
-        await_w(8, 9)
-        g13 = late_of(4, far_end, other, end, me)
+        await_w(16, 17, 18, 19)
+        multiply(*g12)
+        combine(*g12)
         multiply(*g13)
         combine(*g13)
+        finish(*g12)
         finish(*g13)
 
     my_cb = (sub + 1 + head) % 2
@@ -791,7 +823,7 @@
     columns = out_weight.shape[1]
     block = (tokens, columns)
     tiles = columns // TILE
-    pieces = 2 * tiles
+    pieces = SPLIT * tiles
     blocks = tokens // BLOCK
     kinds = 2 * blocks + tiles - EARLY
     anywhere = pl.BlockSpec(memory_space=pl.ANY)
@@ -805,7 +837,7 @@
         out_specs=anywhere,
         scratch_shapes=[
             pltpu.VMEM((n * tokens, 2 * pairs * HD), bf16),
-            pltpu.VMEM((n * tokens, 2 * HD), bf16),
+            pltpu.VMEM((pairs, n * tokens, 2 * HD), bf16),
             pltpu.VMEM((tokens, width), bf16),
             pltpu.VMEM((n, tokens, width), bf16),
             pltpu.VMEM(out_weight.shape, bf16),

time: 146 us -> 130 us (0.89)
  Pallas kernels: 144 us -> 128 us
    pallas_call x1, Pallas kernels: 144 us -> 128 us  [with_hubs(): pl.pallas_call(functools.partial(hub_kernel, n, n_head, per_pair, pairs,...]
where the time goes in v2:
time: 130 us
  Pallas kernels  128 us (98%)
  local copies, waits for them, and re-layouts  2.21 us (2%)
    pallas_call x1, Pallas kernels, with_hubs(): pl.pallas_call(functools.partial(hub_kernel, n, n_head, per_pair, pairs,...  128 us

profile of v2, /device:TPU:0, one launch (start us, length us, event | category | flops | bytes accessed | tf_op | source)
XLA Modules:
  0.0 129.8 jit_solution(9009599796261534549)
XLA Ops:
  0.0 127.6 %shard_map.46 = bf16[384,1280]{1,0:T(8,128)(2,1)} custom-call(bf16[384,512]{1,0:T(8,128)(2,1)} %k_hbm.1, bf16[384,512]{1,0:T(8,128)(2,1)} %v_hbm.1, bf16[384,2048]{1,0:T(8,128)(2,1)} %q_hbm.1, bf16[2048,1280]{1,0:T(8,128)(2,1)} %w_hbm.1), custom_call_target="tpu_custom_call" | custom-call | tf_op jit(solution)/shard_map/pallas_call | solution.py:833
  127.6 2.2 %copy.6 = bf16[384,1280]{1,0:T(8,128)(2,1)} copy(bf16[384,1280]{1,0:T(8,128)(2,1)} %shard_map.46) | data formatting | bytes 1966080

commit v3 on v2

--- a/solution.py
+++ b/solution.py
@@ -19,7 +19,7 @@
 EARLY = 2
 SPLIT = 4
 TOGETHER = 4
-ORDER = ("w",) * 8 + (0, 1, 2) + ("w",) * 12
+ORDER = ("w",) * 8 + (0, 1, 2) + ("w",) * 13
 
 
 def kernel(
@@ -341,9 +341,16 @@
     )(key_rows, value_rows, queries, out_weight)
 
 
+def pieces_of(width, tiles):
+    depth = width // (2 * SPLIT)
+    cuts = [(i, k * depth, depth) for i in range(tiles) for k in range(SPLIT)]
+    at, row, _ = cuts.pop()
+    return cuts + [(at, row, depth // 2), (at, row + depth // 2, depth // 2)]
+
+
 def hub_kernel(
     n, n_head, per_pair, pairs, chunks, tile, k_hbm, v_hbm, q_hbm, w_hbm, o_ref,
-    kv_all, v_ext, q_ref, att, w, w_far, part, rx1, rx2,
+    kv_all, v_ext, q_ref, att, w, w_far, part, rx1, rx2, acc, landing,
     load_sems, kv_send, kv_recv, a_send, a_recv, e_send, e_recv, f_send, f_recv,
     w_send, w_recv, y_send, y_recv, s1, r1, s2, r2, s3, r3,
 ):
@@ -353,8 +360,8 @@
     columns = w.shape[1]
     blocks = tokens // BLOCK
     tiles = columns // tile
-    pieces = SPLIT * tiles
-    per_piece = width // (2 * SPLIT)
+    cuts = pieces_of(width, tiles)
+    pieces = len(cuts)
     low = n // 2 - 1
     is_hub = jnp.logical_and(me >= low, me <= low + 1)
     is_end = jnp.logical_not(is_hub)
@@ -434,8 +441,9 @@
             pl.when(to_left)(lambda: copy.start())
 
     def w_piece(g, i):
-        rows = pl.ds(pl.multiple_of(g * (width // 2) + (i % SPLIT) * per_piece, per_piece), per_piece)
-        return rows, pl.ds((i // SPLIT) * tile, tile)
+        at, row, depth = cuts[i]
+        rows = pl.ds(pl.multiple_of(g * (width // 2) + row, depth), depth)
+        return rows, pl.ds(at * tile, tile)
 
     def w_copy(i):
         at = w_piece(group, i)
@@ -601,6 +609,16 @@
             part.at[t, cb, rows, cols], o_ref.at[rows, cols], s3.at[t // 2, index], r3.at[head, index], where
         )
 
+    def whole_copy(t, kind, r):
+        cb, rows, cols, index = region(kind, r)
+        where = {"ctx": t, "head": side, "sub": (me + cb) % 2}
+        return remote(
+            part.at[t, cb, rows, cols], landing.at[head], s3.at[t // 2, index], r3.at[head, index], where
+        )
+
+    def is_last(kind, r):
+        return kind == "late" and r == tiles - 1
+
     def keep_copy(t, kind, r):
         cb, rows, cols, index = region(kind, r, head)
         return pltpu.make_async_copy(part.at[t, cb, rows, cols], o_ref.at[rows, cols], s3.at[t // 2, index])
@@ -616,6 +634,29 @@
         for t, kind, r in jobs:
             cb, row, m, c, k, _ = geometry(kind, r)
             product(t, row, m, cb, c, k)
+            send([(t, kind, r)])
+
+    def slab(t, k):
+        last = pl.ds((tiles - 1) * tile, tile)
+        total = None
+        for g in range(2):
+            depth = pl.ds(g * (width // 2) + k * (width // 2 // SPLIT), width // 2 // SPLIT)
+            term = jnp.dot(att[t, :, depth], w_far[depth, last], preferred_element_type=jnp.float32)
+            total = term if total is None else total + term
+        return total
+
+    def begin(*toks):
+        for t in toks:
+            acc[t] = slab(t, 0) + slab(t, 1)
+
+    def extend(*toks):
+        for t in toks:
+            acc[t] += slab(t, 2)
+
+    def complete(*jobs):
+        for t, kind, r in jobs:
+            total = acc[t] + slab(t, 3)
+            part[t, 1, :, pl.ds((tiles - 1) * tile, tile)] = total.astype(part.dtype)
             send([(t, kind, r)])
 
     def multiply_all(t, kind):
@@ -633,7 +674,7 @@
                 total = part[t, cb, rows, cols].astype(jnp.float32)
                 total += rx1[t // 2, cb, rows, cols].astype(jnp.float32)
                 part[t, cb, rows, cols] = total.astype(part.dtype)
-                head_copy(t, kind, r).start()
+                (whole_copy if is_last(kind, r) else head_copy)(t, kind, r).start()
 
     def finish(*jobs):
         for t, kind, r in jobs:
@@ -724,49 +765,32 @@
         finish(*g9)
         await_far(2)
         relay_w(14)
-        multiply(*g11)
+        multiply(*g11[:2])
         relay_w(15)
+        multiply(*g11[2:])
         combine(*g11)
         finish(*g7)
         relay_w(16)
+        relay_w(17)
         await_w(12, 13, 14, 15)
         multiply(*g10[:2])
-        relay_w(17)
+        relay_w(18)
         multiply(*g10[2:])
-        relay_w(18)
+        relay_w(19)
         combine(*g10)
+        relay_w(20)
         finish(*g8)
         finish(*g11)
-        relay_w(19)
+        await_w(16, 17)
+        begin(far_end, other, end, me)
+        await_w(18)
+        extend(far_end, other, end, me)
         finish(*g10)
-        await_w(16, 17, 18, 19)
-        multiply(*g12)
+        await_w(19, 20)
+        complete(*g12)
+        complete(*g13)
         combine(*g12)
-        multiply(*g13)
         combine(*g13)
-        finish(*g12)
-        finish(*g13)
-
-    my_cb = (sub + 1 + head) % 2
-
-    def arrivals(cb):
-        kinds = [("near", r) for r in range(blocks)]
-        if cb:
-            kinds = [("early", r) for r in range(blocks)] + [("late", r) for r in range(EARLY, tiles)]
-        for kind, r in kinds:
-            for h in range(n_head):
-                cb_, rows, cols, index = region(kind, r, h)
-                got = remote(
-                    part.at[0, cb_, rows, cols], o_ref.at[rows, cols], s3.at[0, index], r3.at[h, index],
-                    {"ctx": origin, "head": h, "sub": me % 2},
-                )
-                if cb:
-                    got.wait_recv()
-                else:
-                    pl.when(jnp.logical_not(jnp.logical_and(mine, head == h)))(lambda: got.wait_recv())
-
-    pl.when(my_cb == 0)(lambda: arrivals(0))
-    pl.when(my_cb == 1)(lambda: arrivals(1))
 
     for way, go in ((0, to_right), (1, to_left)):
         for d in range(n):
@@ -800,6 +824,9 @@
 
                 @pl.when(owns(t))
                 def _():
+                    if is_last(kind, r):
+                        whole_copy(t, kind, r).wait_send()
+                        return
                     head_copy(t, kind, r).wait_send()
                     if kind == "near":
                         kept = is_kept(t, 0)
@@ -811,6 +838,41 @@
                 @pl.when(jnp.logical_not(owns(t)))
                 def _():
                     core_copy(t, kind, r).wait_send()
+
+    my_cb = (sub + 1 + head) % 2
+
+    def arrivals(cb):
+        kinds = [("near", r) for r in range(blocks)]
+        if cb:
+            kinds = [("early", r) for r in range(blocks)] + [("late", r) for r in range(EARLY, tiles - 1)]
+        for kind, r in kinds:
+            for h in range(n_head):
+                cb_, rows, cols, index = region(kind, r, h)
+                got = remote(
+                    part.at[0, cb_, rows, cols], o_ref.at[rows, cols], s3.at[0, index], r3.at[h, index],
+                    {"ctx": origin, "head": h, "sub": me % 2},
+                )
+                if cb:
+                    got.wait_recv()
+                else:
+                    pl.when(jnp.logical_not(jnp.logical_and(mine, head == h)))(lambda: got.wait_recv())
+        if cb:
+            cb_, rows, cols, index = region("late", tiles - 1)
+            for h in range(n_head):
+                remote(
+                    part.at[0, cb_, rows, cols], landing.at[h], s3.at[0, index], r3.at[h, index],
+                    {"ctx": origin, "head": h, "sub": me % 2},
+                ).wait_recv()
+            total = landing[0].astype(jnp.float32)
+            for h in range(1, n_head):
+                total += landing[h].astype(jnp.float32)
+            landing[0] = total.astype(landing.dtype)
+            place = pltpu.make_async_copy(landing.at[0], o_ref.at[rows, cols], load_sems.at[0])
+            place.start()
+            place.wait()
+
+    pl.when(my_cb == 0)(lambda: arrivals(0))
+    pl.when(my_cb == 1)(lambda: arrivals(1))
 
 
 def with_hubs(queries, key_rows, value_rows, out_weight):
@@ -823,7 +885,7 @@
     columns = out_weight.shape[1]
     block = (tokens, columns)
     tiles = columns // TILE
-    pieces = SPLIT * tiles
+    pieces = len(pieces_of(width, tiles))
     blocks = tokens // BLOCK
     kinds = 2 * blocks + tiles - EARLY
     anywhere = pl.BlockSpec(memory_space=pl.ANY)
@@ -845,6 +907,8 @@
             pltpu.VMEM((n, 2) + block, bf16),
             pltpu.VMEM((n // 2, 2) + block, bf16),
             pltpu.VMEM((n // 2, 2, tokens // 2, columns), bf16),
+            pltpu.VMEM((n, tokens, TILE), jnp.float32),
+            pltpu.VMEM((n_head, tokens, TILE), bf16),
             dma((2 * pairs + 2,)),
             dma((2, n, pairs)),
             dma((n, pairs)),

time: 130 us -> 125 us (0.962)
  Pallas kernels: 128 us -> 122 us
    pallas_call x1, Pallas kernels: 128 us -> 122 us  [with_hubs(): pl.pallas_call(functools.partial(hub_kernel, n, n_head, per_pair, pairs,...]
where the time goes in v3:
time: 125 us
  Pallas kernels  122 us (98%)
  local copies, waits for them, and re-layouts  2.21 us (2%)
    pallas_call x1, Pallas kernels, with_hubs(): pl.pallas_call(functools.partial(hub_kernel, n, n_head, per_pair, pairs,...  122 us

profile of v3, /device:TPU:0, one launch (start us, length us, event | category | flops | bytes accessed | tf_op | source)
XLA Modules:
  0.0 124.7 jit_solution(10821581295126074715)
XLA Ops:
  0.0 122.5 %shard_map.46 = bf16[384,1280]{1,0:T(8,128)(2,1)} custom-call(bf16[384,512]{1,0:T(8,128)(2,1)} %k_hbm.1, bf16[384,512]{1,0:T(8,128)(2,1)} %v_hbm.1, bf16[384,2048]{1,0:T(8,128)(2,1)} %q_hbm.1, bf16[2048,1280]{1,0:T(8,128)(2,1)} %w_hbm.1), custom_call_target="tpu_custom_call" | custom-call | tf_op jit(solution)/shard_map/pallas_call | solution.py:895
  122.5 2.2 %copy.6 = bf16[384,1280]{1,0:T(8,128)(2,1)} copy(bf16[384,1280]{1,0:T(8,128)(2,1)} %shard_map.46) | data formatting | bytes 1966080

commit v4 on v3

--- a/solution.py
+++ b/solution.py
@@ -759,12 +759,12 @@
         finish(*g6)
         relay_w(12)
         await_w(8, 9, 10, 11)
+        relay_w(13)
         multiply(*g8)
-        relay_w(13)
+        relay_w(14)
         combine(*g8)
         finish(*g9)
         await_far(2)
-        relay_w(14)
         multiply(*g11[:2])
         relay_w(15)
         multiply(*g11[2:])
@@ -775,22 +775,25 @@
         await_w(12, 13, 14, 15)
         multiply(*g10[:2])
         relay_w(18)
-        multiply(*g10[2:])
+        combine(*g10[:2])
+        multiply(*g10[2:3])
         relay_w(19)
-        combine(*g10)
+        multiply(*g10[3:])
+        combine(*g10[2:])
         relay_w(20)
         finish(*g8)
         finish(*g11)
         await_w(16, 17)
         begin(far_end, other, end, me)
+        finish(*g10[:2])
         await_w(18)
         extend(far_end, other, end, me)
-        finish(*g10)
         await_w(19, 20)
         complete(*g12)
         complete(*g13)
         combine(*g12)
         combine(*g13)
+        finish(*g10[2:])
 
     for way, go in ((0, to_right), (1, to_left)):
         for d in range(n):

time: 125 us -> 127 us (1.016)
  Pallas kernels: 122 us -> 124 us
    pallas_call x1, Pallas kernels: 122 us -> 124 us  [with_hubs(): pl.pallas_call(functools.partial(hub_kernel, n, n_head, per_pair, pairs,...]
where the time goes in v4:
time: 127 us
  Pallas kernels  124 us (98%)
  local copies, waits for them, and re-layouts  2.21 us (2%)
    pallas_call x1, Pallas kernels, with_hubs(): pl.pallas_call(functools.partial(hub_kernel, n, n_head, per_pair, pairs,...  124 us

profile of v4, /device:TPU:0, one launch (start us, length us, event | category | flops | bytes accessed | tf_op | source)
XLA Modules:
  0.0 126.6 jit_solution(5571942614026294938)
XLA Ops:
  0.0 124.4 %shard_map.46 = bf16[384,1280]{1,0:T(8,128)(2,1)} custom-call(bf16[384,512]{1,0:T(8,128)(2,1)} %k_hbm.1, bf16[384,512]{1,0:T(8,128)(2,1)} %v_hbm.1, bf16[384,2048]{1,0:T(8,128)(2,1)} %q_hbm.1, bf16[2048,1280]{1,0:T(8,128)(2,1)} %w_hbm.1), custom_call_target="tpu_custom_call" | custom-call | tf_op jit(solution)/shard_map/pallas_call | solution.py:898
  124.4 2.2 %copy.6 = bf16[384,1280]{1,0:T(8,128)(2,1)} copy(bf16[384,1280]{1,0:T(8,128)(2,1)} %shard_map.46) | data formatting | bytes 1966080

commit v5 on v3

--- a/solution.py
+++ b/solution.py
@@ -759,12 +759,12 @@
         finish(*g6)
         relay_w(12)
         await_w(8, 9, 10, 11)
+        relay_w(13)
         multiply(*g8)
-        relay_w(13)
+        relay_w(14)
         combine(*g8)
         finish(*g9)
         await_far(2)
-        relay_w(14)
         multiply(*g11[:2])
         relay_w(15)
         multiply(*g11[2:])

time: 125 us -> 126 us (level)
  no operation moved by 1% of the time
where the time goes in v5:
time: 126 us
  Pallas kernels  123 us (98%)
  local copies, waits for them, and re-layouts  2.21 us (2%)
    pallas_call x1, Pallas kernels, with_hubs(): pl.pallas_call(functools.partial(hub_kernel, n, n_head, per_pair, pairs,...  123 us

profile of v5, /device:TPU:0, one launch (start us, length us, event | category | flops | bytes accessed | tf_op | source)
XLA Modules:
  0.0 125.6 jit_solution(7981739302206002137)
XLA Ops:
  0.0 123.4 %shard_map.46 = bf16[384,1280]{1,0:T(8,128)(2,1)} custom-call(bf16[384,512]{1,0:T(8,128)(2,1)} %k_hbm.1, bf16[384,512]{1,0:T(8,128)(2,1)} %v_hbm.1, bf16[384,2048]{1,0:T(8,128)(2,1)} %q_hbm.1, bf16[2048,1280]{1,0:T(8,128)(2,1)} %w_hbm.1), custom_call_target="tpu_custom_call" | custom-call | tf_op jit(solution)/shard_map/pallas_call | solution.py:895
  123.4 2.2 %copy.6 = bf16[384,1280]{1,0:T(8,128)(2,1)} copy(bf16[384,1280]{1,0:T(8,128)(2,1)} %shard_map.46) | data formatting | bytes 1966080
